TPU v7x, 128 devices: a whole 4x4x4 slice. The times are simulated.
128 devices in a mesh: px: 8 (over x, core), py: 16 (over y, z).
Axes of the slice: x: 4, y: 4, z: 4, core: 2. Of those that a mesh axis runs over, the one named last changes fastest.
Arguments:
- root_density: float32 [384, 384, 384], P('px', 'py'), may hold values from -6 to 6
- subgrid_density: float32 [2048, 32, 1024], P(('px', 'py')), may hold values from -24 to 24
- velocity: float32 [3, 2048, 32, 1024], P(None, ('px', 'py')), may hold values from -6 to 6
- slot_anchor: int32 [3, 2048], replicated, may hold values from 0 to 376, as said below
- slot_count: int32 [128], replicated, may hold values from 1 to 16, as said below
- neighbour: int32 [2, 2048], replicated, may hold values from -1 to 2047, as said below
Outputs:
- coarse_potential: float32 [384, 384, 384], P('px', 'py')
- subgrid_potential: float32 [2048, 32, 1024], P(('px', 'py'))
- kicked_velocity: float32 [3, 2048, 32, 1024], P(None, ('px', 'py'))
Inputs may be any that keep to these rules, and one draw needn't show every extreme that they name: Slot j of device d is slot d * 16 + j, devices numbered in the order of px+py; it is live when j < slot_count[d]. Some device has every slot live. `slot_anchor`: entries are multiples of 8; live slots cover distinct regions of 8^3 root cells; empty slots hold 0. The region of live slot j of the device at px = p, py = q has its lower corner among the root cells that the device at px = p, py = (q + j) mod 16 holds of root_density. neighbour[0, s] is s - 16 or -1 and neighbour[1, s] is s + 16 or -1, the same slot of the device one index lower or higher along py with the same px; where set, both slots are live and the two regions lie next to each other along the second dimension, the lower one below. Empty slots hold -1.
All inputs are finite; a program needn't handle non-finite values.
Results may differ from a plain program's by a relative error of at most 0.000094.
Values sent between devices are 32-bit elements; how exact they have to be, the bound alone decides.
No kernel may reach another device: no remote copies, remote signals or barrier semaphores. Data moves between devices by JAX's collectives and lax.ppermute only.
A program may use at most 128 MiB of HBM per device.

v0:
```python
import jax
import jax.numpy as jnp
from jax import lax
from jax.sharding import PartitionSpec as P

NR = 384
REG = 8
REF = 4
SWEEPS = 4
HIGHEST_PRECISION = lax.Precision.HIGHEST
RELAXATION = 6.0 / 7.0
EINSUM_FORMS = ("abc,ad->dbc", "abc,bd->adc", "abc,cd->abd")


def from_behind(value, axis, steps):
    count = lax.axis_size(axis)
    initial, last = (max(0, -steps), min(count, count - steps))
    return lax.ppermute(value, axis, [(source, source + steps) for source in range(initial, last)])


def extended(block, sides, width):
    for axis, dim in sides:
        count = lax.axis_size(axis)
        forward = [(i, i + 1) for i in range(count - 1)]
        forward.append((count - 1, 0))
        backward = [(target, source) for source, target in forward]
        low = lax.ppermute(
            lax.slice_in_dim(block, block.shape[dim] - width, None, axis=dim), axis, forward
        )
        high = lax.ppermute(lax.slice_in_dim(block, 0, width, axis=dim), axis, backward)
        block = jnp.concatenate([low, block, high], axis=dim)
    return block


def tables(length):
    positions = jnp.arange(length, dtype=jnp.int32)
    angle_table = (
        2.0
        * jnp.pi
        / length
        * (positions[:, None] * positions[None, :] % length).astype(jnp.float32)
    )
    return (jnp.cos(angle_table), jnp.sin(angle_table))


def transform_along(values_in, matrix, axis_number):
    return jnp.einsum(EINSUM_FORMS[axis_number], values_in, matrix, precision=HIGHEST_PRECISION)


def forward(complex_pair, axis_number, cosine_table, sine_table):
    real_part, imag_part = complex_pair
    return (
        transform_along(real_part, cosine_table, axis_number)
        + transform_along(imag_part, sine_table, axis_number),
        transform_along(imag_part, cosine_table, axis_number)
        - transform_along(real_part, sine_table, axis_number),
    )


def inverse(complex_pair, axis_number, cosine_table, sine_table):
    real_part, imag_part = complex_pair
    scale_factor = 1.0 / cosine_table.shape[0]
    return (
        (
            transform_along(real_part, cosine_table, axis_number)
            - transform_along(imag_part, sine_table, axis_number)
        )
        * scale_factor,
        (
            transform_along(imag_part, cosine_table, axis_number)
            + transform_along(real_part, sine_table, axis_number)
        )
        * scale_factor,
    )


def eigenvalue(wavenumber):
    return -4.0 * jnp.sin(jnp.pi / NR * wavenumber.astype(jnp.float32)) ** 2


def green_block(wave_first, wave_second, wave_third):
    total = (
        eigenvalue(wave_first)[:, None, None]
        + eigenvalue(wave_second)[None, :, None]
        + eigenvalue(wave_third)[None, None, :]
    )
    zero_mode = (
        (wave_first[:, None, None] == 0)
        & (wave_second[None, :, None] == 0)
        & (wave_third[None, None, :] == 0)
    )
    safe_total = jnp.where(zero_mode, -1.0, total)
    return jnp.where(zero_mode, 0.0, 1.0 / safe_total)


def weights_table():
    cells = jnp.arange(REG * REF + 2, dtype=jnp.int32)
    marks = 2 * cells - 1 + REF
    lower_cell = jnp.minimum(marks // (2 * REF), REG)
    fraction = (marks - 2 * REF * lower_cell).astype(jnp.float32) / (2 * REF)
    columns = jnp.arange(REG + 2, dtype=jnp.int32)
    return jnp.where(
        columns[None, :] == lower_cell[:, None], 1.0 - fraction[:, None], 0.0
    ) + jnp.where(columns[None, :] == lower_cell[:, None] + 1, fraction[:, None], 0.0)


def coarse_parts(patch_flat, weights):
    inner = weights[1:-1]
    cells = inner.shape[0]
    width = weights.shape[1]
    both_inner = jnp.einsum("jb,kc->jkbc", inner, inner, precision=HIGHEST_PRECISION).reshape(
        cells * cells, width * width
    )
    second_low = jnp.einsum("b,kc->kbc", weights[0], inner, precision=HIGHEST_PRECISION).reshape(
        cells, width * width
    )
    second_high = jnp.einsum("b,kc->kbc", weights[-1], inner, precision=HIGHEST_PRECISION).reshape(
        cells, width * width
    )
    third_low = jnp.einsum("jb,c->jbc", inner, weights[0], precision=HIGHEST_PRECISION).reshape(
        cells, width * width
    )
    third_high = jnp.einsum("jb,c->jbc", inner, weights[-1], precision=HIGHEST_PRECISION).reshape(
        cells, width * width
    )
    plane_values = jnp.einsum("sam,nm->san", patch_flat, both_inner, precision=HIGHEST_PRECISION)
    interior = jnp.einsum("san,ia->sin", plane_values, inner, precision=HIGHEST_PRECISION)
    first_low_face = jnp.einsum("san,a->sn", plane_values, weights[0], precision=HIGHEST_PRECISION)
    first_high_face = jnp.einsum(
        "san,a->sn", plane_values, weights[-1], precision=HIGHEST_PRECISION
    )

    def face_of(table):
        partial_face = jnp.einsum("sam,km->sak", patch_flat, table, precision=HIGHEST_PRECISION)
        return jnp.einsum("sak,ia->sik", partial_face, inner, precision=HIGHEST_PRECISION)

    return (
        interior,
        first_low_face,
        first_high_face,
        face_of(second_low),
        face_of(second_high),
        face_of(third_low),
        face_of(third_high),
    )


def spread_third(face_values, cells, corner):
    positions = jnp.arange(cells * cells, dtype=jnp.int32)
    rows = jnp.arange(cells, dtype=jnp.int32)
    placer = (positions[None, :] == rows[:, None] * cells + corner).astype(jnp.float32)
    return jnp.einsum("sij,jn->sin", face_values, placer, precision=HIGHEST_PRECISION)


def beside_values(interior, first_faces, second_faces, third_full, third_place):
    cells = interior.shape[1]
    slots = interior.shape[0]
    first_low, first_high = first_faces
    second_low, second_high = second_faces
    third_low, third_high = third_full
    below_first = jnp.concatenate([first_low[:, None, :], interior[:, :-1]], axis=1)
    above_first = jnp.concatenate([interior[:, 1:], first_high[:, None, :]], axis=1)
    below_second = jnp.concatenate([second_low, interior[:, :, :-cells]], axis=2)
    above_second = jnp.concatenate([interior[:, :, cells:], second_high], axis=2)
    zero_column = jnp.zeros((slots, cells, 1), jnp.float32)
    below_third = jnp.where(
        third_place == 0, third_low, jnp.concatenate([zero_column, interior[:, :, :-1]], axis=2)
    )
    above_third = jnp.where(
        third_place == cells - 1,
        third_high,
        jnp.concatenate([interior[:, :, 1:], zero_column], axis=2),
    )
    return ((below_first, above_first), (below_second, above_second), (below_third, above_third))


def cut_patches(padded, anchors, corner_first, corner_second):
    offsets = jnp.arange(REG + 2, dtype=jnp.int32)
    index_first = jnp.clip(
        anchors[0][:, None] - corner_first + offsets[None, :], 0, padded.shape[0] - 1
    )
    index_second = jnp.clip(
        anchors[1][:, None] - corner_second + offsets[None, :], 0, padded.shape[1] - 1
    )
    index_third = (anchors[2][:, None] - 1 + offsets[None, :]) % NR
    picked = padded[
        index_first[:, :, None, None], index_second[:, None, :, None], index_third[:, None, None, :]
    ]
    return picked.reshape(anchors.shape[1], -1)


def neighbour_faces(interior):
    cells = interior.shape[1]
    top_layer = interior[:, :, (cells - 1) * cells :]
    bottom_layer = interior[:, :, :cells]
    from_below = from_behind(top_layer, "py", 1)
    from_above = from_behind(bottom_layer, "py", -1)
    return (from_below, from_above)


def local(root_density, subgrid_density, velocity, slot_anchor, slot_count, neighbour):
    cosine_table, sine_table = tables(NR)
    first_rows = root_density.shape[0]
    second_rows = root_density.shape[1]
    size_second = lax.axis_size("py")
    place_first = lax.axis_index("px")
    place_second = lax.axis_index("py")
    device = place_first * size_second + place_second
    every_wave = jnp.arange(NR, dtype=jnp.int32)
    real_part = transform_along(root_density, cosine_table, 2)
    imag_part = -transform_along(root_density, sine_table, 2)
    spectrum = (
        lax.all_to_all(real_part, "py", split_axis=0, concat_axis=1, tiled=True),
        lax.all_to_all(imag_part, "py", split_axis=0, concat_axis=1, tiled=True),
    )
    spectrum = forward(spectrum, 1, cosine_table, sine_table)
    spectrum = (
        lax.all_to_all(spectrum[0], ("px", "py"), split_axis=1, concat_axis=0, tiled=True),
        lax.all_to_all(spectrum[1], ("px", "py"), split_axis=1, concat_axis=0, tiled=True),
    )
    band = spectrum[0].shape[1]
    band_start = device * band
    spectrum = forward(spectrum, 0, cosine_table, sine_table)
    factor = green_block(every_wave, band_start + jnp.arange(band, dtype=jnp.int32), every_wave)
    spectrum = inverse((spectrum[0] * factor, spectrum[1] * factor), 0, cosine_table, sine_table)
    spectrum = (
        lax.all_to_all(spectrum[0], ("px", "py"), split_axis=0, concat_axis=1, tiled=True),
        lax.all_to_all(spectrum[1], ("px", "py"), split_axis=0, concat_axis=1, tiled=True),
    )
    spectrum = inverse(spectrum, 1, cosine_table, sine_table)
    spectrum = (
        lax.all_to_all(spectrum[0], "py", split_axis=1, concat_axis=0, tiled=True),
        lax.all_to_all(spectrum[1], "py", split_axis=1, concat_axis=0, tiled=True),
    )
    coarse_potential = (
        transform_along(spectrum[0], cosine_table, 2) - transform_along(spectrum[1], sine_table, 2)
    ) * (1.0 / NR)
    per_device = subgrid_density.shape[0]
    cells = subgrid_density.shape[1]
    positions = jnp.arange(per_device, dtype=jnp.int32)
    corner_first = place_first * first_rows
    corner_second = place_second * second_rows
    padded = extended(coarse_potential, (("px", 0), ("py", 1)), 1)
    targets = jnp.arange(size_second, dtype=jnp.int32)
    owner_devices = place_first * size_second + targets
    wanted_slot = (place_second - targets) % size_second
    global_slot = owner_devices * per_device + wanted_slot
    sending_live = wanted_slot < slot_count[owner_devices]
    sending = cut_patches(padded, slot_anchor[:, global_slot], corner_first, corner_second)
    sending = jnp.where(sending_live[:, None], sending, 0.0)
    arrived = lax.all_to_all(sending, "py", split_axis=0, concat_axis=0, tiled=True)
    patch = arrived[(place_second + positions) % size_second]
    patch_flat = patch.reshape(per_device, REG + 2, (REG + 2) * (REG + 2))
    interior, first_low, first_high, second_low, second_high, third_low, third_high = coarse_parts(
        patch_flat, weights_table()
    )
    third_full = (spread_third(third_low, cells, 0), spread_third(third_high, cells, cells - 1))
    third_place = jnp.arange(cells * cells, dtype=jnp.int32) % cells
    own_live = positions < slot_count[device]
    first_slot = device * per_device
    nearby = lax.dynamic_slice_in_dim(neighbour, first_slot, per_device, 1)
    use_below = (nearby[0] >= 0)[:, None, None]
    use_above = (nearby[1] >= 0)[:, None, None]

    def all_beside(current):
        from_below, from_above = neighbour_faces(current)
        second_faces = (
            jnp.where(use_below, from_below, second_low),
            jnp.where(use_above, from_above, second_high),
        )
        return beside_values(
            current, (first_low, first_high), second_faces, third_full, third_place
        )

    for sweep_index in range(SWEEPS):
        along_first, along_second, along_third = all_beside(interior)
        beside_all = (
            along_first[1]
            + along_first[0]
            + along_second[1]
            + along_second[0]
            + along_third[1]
            + along_third[0]
        )
        interior = (1.0 - RELAXATION) * interior + RELAXATION * (
            beside_all - subgrid_density * (1.0 / (REF * REF))
        ) / 6.0
    along_first, along_second, along_third = all_beside(interior)
    scale_factor = REF / 2.0
    slopes = jnp.stack(
        [
            (along_first[1] - along_first[0]) * scale_factor,
            (along_second[1] - along_second[0]) * scale_factor,
            (along_third[1] - along_third[0]) * scale_factor,
        ]
    )
    subgrid_potential = jnp.where(own_live[:, None, None], interior, 0.0)
    velocity_after_kick = jnp.where(own_live[None, :, None, None], velocity - slopes, 0.0)
    return (coarse_potential, subgrid_potential, velocity_after_kick)


def solution(mesh):
    return jax.shard_map(
        local,
        mesh=mesh,
        in_specs=(
            P("px", "py", None),
            P(("px", "py"), None, None),
            P(None, ("px", "py"), None, None),
            P(),
            P(),
            P(),
        ),
        out_specs=(
            P("px", "py", None),
            P(("px", "py"), None, None),
            P(None, ("px", "py"), None, None),
        ),
        check_vma=False,
    )
```

profile of v0, /device:TPU:96, one launch (start us, length us, event | category | flops | bytes accessed | tf_op | source)
XLA Modules:
  0.0 679.2 jit_solution(3072733215062630244)
XLA Ops:
  2.1 5.8 negate_bitcast_fusion
  9.6 7.8 %all-to-all-start.1 = ((f32[48,24,384]{2,1,0:T(8,128)}), f32[48,24,384]{2,1,0:T(8,128)S(1)}, u32[]{:S(2)}, u32[]{:S(2)}) async-start(f32[48,24,384]{2,1,0:T(8,128)} %copy.93), calls=%async_computation.1 | async-start | bytes 3538944 | tf_op jit(solution)/shard_map/all_to_all | solution.py:214
  17.4 5.8 fusion.38
  24.9 15.3 %all-to-all-done.1 = f32[48,24,384]{2,1,0:T(8,128)S(1)} async-done(((f32[48,24,384]{2,1,0:T(8,128)}), f32[48,24,384]{2,1,0:T(8,128)S(1)}, u32[]{:S(2)}, u32[]{:S(2)}) %all-to-all-start.1) | async-done | bytes 1769504 | tf_op jit(solution)/shard_map/all_to_all | solution.py:214
  40.2 7.7 %all-to-all-start = ((f32[48,24,384]{2,1,0:T(8,128)}), f32[48,24,384]{2,1,0:T(8,128)}, u32[]{:S(2)}, u32[]{:S(2)}) async-start(f32[48,24,384]{2,1,0:T(8,128)} %copy.89), calls=%async_computation | async-start | bytes 3538944 | tf_op jit(solution)/shard_map/all_to_all | solution.py:213
  48.1 21.4 %all-to-all-done = f32[48,24,384]{2,1,0:T(8,128)} async-done(((f32[48,24,384]{2,1,0:T(8,128)}), f32[48,24,384]{2,1,0:T(8,128)}, u32[]{:S(2)}, u32[]{:S(2)}) %all-to-all-start) | async-done | bytes 1769504 | tf_op jit(solution)/shard_map/all_to_all | solution.py:213
  71.0 5.3 fusion.71
  76.3 5.4 add_bitcast_fusion
  84.7 9.3 %all-to-all-start.2 = ((f32[3,384,384]{2,0,1:T(4,128)}), f32[3,384,384]{2,0,1:T(4,128)}, u32[]{:S(2)}, u32[]{:S(2)}) async-start(f32[3,384,384]{2,0,1:T(4,128)} %copy.96), calls=%async_computation.2 | async-start | bytes 4718592 | tf_op jit(solution)/shard_map/all_to_all | solution.py:218
  94.1 5.3 fusion.66
  99.4 5.4 subtract_bitcast_fusion
  107.6 17.3 %all-to-all-done.2 = f32[3,384,384]{2,0,1:T(4,128)} async-done(((f32[3,384,384]{2,0,1:T(4,128)}), f32[3,384,384]{2,0,1:T(4,128)}, u32[]{:S(2)}, u32[]{:S(2)}) %all-to-all-start.2) | async-done | bytes 1769504 | tf_op jit(solution)/shard_map/all_to_all | solution.py:218
  124.8 6.2 all-to-all-start.3
  134.8 4.1 all_to_all.121
  138.9 23.2 %all-to-all-done.3 = f32[3,384,384]{2,0,1:T(4,128)S(1)} async-done(((f32[3,384,384]{2,0,1:T(4,128)}), f32[3,384,384]{2,0,1:T(4,128)S(1)}, u32[]{:S(2)}, u32[]{:S(2)}) %all-to-all-start.3) | async-done | bytes 1769504 | tf_op jit(solution)/shard_map/all_to_all | solution.py:219
  166.7 5.3 fusion.64
  172.1 5.3 fusion.73
  177.4 6.2 subtract_multiply_fusion.2
  183.6 5.8 add_multiply_fusion.1
  189.4 5.5 fusion.62
  194.9 5.4 add_multiply_fusion
  202.9 6.6 all-to-all-start.5
  209.5 6.9 %fusion.75 = f32[384,3,384]{2,0,1:T(8,128)S(1)} fusion(f32[384,3,384]{2,0,1:T(8,128)} %copy-done.8), kind=kOutput, calls=%fused_computation.115 | convolution fusion | flops 2039758848 | bytes 3538944 | tf_op jit(solution)/shard_map/abc,ad->dbc/dot_general | solution.py:47
  216.4 5.4 subtract_multiply_fusion.1
  224.6 15.5 %all-to-all-done.5 = f32[384,3,384]{2,1,0:T(4,128)S(1)} async-done(((f32[384,3,384]{2,1,0:T(4,128)}), f32[384,3,384]{2,1,0:T(4,128)S(1)}, u32[]{:S(2)}, u32[]{:S(2)}) %all-to-all-start.5) | async-done | bytes 1769504 | tf_op jit(solution)/shard_map/all_to_all | solution.py:228
  240.1 7.0 %all-to-all-start.4 = ((f32[384,3,384]{2,1,0:T(4,128)}), f32[384,3,384]{2,1,0:T(4,128)}, u32[]{:S(2)}, u32[]{:S(2)}) async-start(f32[384,3,384]{2,1,0:T(4,128)} %copy.110), calls=%async_computation.4 | async-start | bytes 4718592 | tf_op jit(solution)/shard_map/all_to_all | solution.py:227
  255.7 22.1 %all-to-all-done.4 = f32[384,3,384]{2,1,0:T(4,128)} async-done(((f32[384,3,384]{2,1,0:T(4,128)}), f32[384,3,384]{2,1,0:T(4,128)}, u32[]{:S(2)}, u32[]{:S(2)}) %all-to-all-start.4) | async-done | bytes 1769504 | tf_op jit(solution)/shard_map/all_to_all | solution.py:227
  284.2 5.3 fusion.60
  289.5 5.4 multiply_bitcast_fusion.1
  297.9 5.9 all-to-all-start.7
  309.2 5.3 fusion.77
  314.5 5.4 multiply_bitcast_fusion.2
  322.7 11.2 %all-to-all-done.7 = f32[3,384,384]{2,0,1:T(4,128)} async-done(((f32[3,384,384]{2,0,1:T(4,128)}), f32[3,384,384]{2,0,1:T(4,128)}, u32[]{:S(2)}, u32[]{:S(2)}) %all-to-all-start.7) | async-done | bytes 1769504 | tf_op jit(solution)/shard_map/all_to_all | solution.py:233
  333.9 6.9 %all-to-all-start.6 = ((f32[3,384,384]{2,0,1:T(4,128)}), f32[3,384,384]{2,0,1:T(4,128)S(1)}, u32[]{:S(2)}, u32[]{:S(2)}) async-start(f32[3,384,384]{2,0,1:T(4,128)} %copy.120), calls=%async_computation.6 | async-start | bytes 4718592 | tf_op jit(solution)/shard_map/all_to_all | solution.py:232
  348.4 20.7 %all-to-all-done.6 = f32[3,384,384]{2,0,1:T(4,128)S(1)} async-done(((f32[3,384,384]{2,0,1:T(4,128)}), f32[3,384,384]{2,0,1:T(4,128)S(1)}, u32[]{:S(2)}, u32[]{:S(2)}) %all-to-all-start.6) | async-done | bytes 1769504 | tf_op jit(solution)/shard_map/all_to_all | solution.py:232
  369.2 5.8 fusion.68
  375.0 6.3 subtract_multiply_fusion
  402.2 151.5 %gather_fusion.2 = f32[16000]{0:T(1024)S(1)} fusion(f32[50,26,384]{2,1,0:T(8,128)S(1)} %pad_maximum_fusion.8, s32[16000]{0:T(1024)S(1)} %reshape.573), kind=kCustom, calls=%fused_computation.2 | custom fusion | bytes 320000 | tf_op jit(solution)/shard_map/gather | solution.py:186
  554.6 9.3 %all-to-all-start.8 = ((f32[16,1,1000]{2,1,0:T(1,128)}), f32[16,1,1000]{2,1,0:T(1,128)S(1)}, u32[]{:S(2)}, u32[]{:S(2)}) async-start(f32[16,1,1000]{2,1,0:T(1,128)} %broadcast_select_fusion.1), calls=%async_computation.8 | async-start | bytes 131072 | tf_op jit(solution)/shard_map/all_to_all | solution.py:251
  564.5 5.1 all-to-all-done.8
  584.9 5.5 collective-permute-start.5
  599.0 6.5 collective-permute-start.7
  609.4 7.3 %collective-permute-done.6 = f32[16,32,32]{2,1,0:T(8,128)S(1)} collective-permute-done((f32[16,32,32]{2,1,0:T(8,128)S(1)}, f32[16,32,32]{2,1,0:T(8,128)S(1)}, u32[]{:S(2)}, u32[]{:S(2)}) %collective-permute-start.6) | collective-permute-done | bytes 65568 | tf_op jit(solution)/shard_map/ppermute | solution.py:18
  623.9 6.0 collective-permute-start.9
  641.0 6.7 collective-permute-start.11
  651.4 4.0 broadcast_select_fusion
  657.7 6.5 collective-permute-start.13
  668.2 6.4 collective-permute-done.12
  (213 shorter events, 142.2 us)
Async XLA Ops:
  9.6 30.6 %all-to-all-start.1 = ((f32[48,24,384]{2,1,0:T(8,128)}), f32[48,24,384]{2,1,0:T(8,128)S(1)}, u32[]{:S(2)}, u32[]{:S(2)}) async-start(f32[48,24,384]{2,1,0:T(8,128)} %copy.93), calls=%async_computation.1 | async-start | bytes 3538944 | tf_op jit(solution)/shard_map/all_to_all | solution.py:214
  40.2 29.3 %all-to-all-start = ((f32[48,24,384]{2,1,0:T(8,128)}), f32[48,24,384]{2,1,0:T(8,128)}, u32[]{:S(2)}, u32[]{:S(2)}) async-start(f32[48,24,384]{2,1,0:T(8,128)} %copy.89), calls=%async_computation | async-start | bytes 3538944 | tf_op jit(solution)/shard_map/all_to_all | solution.py:213
  84.7 40.1 %all-to-all-start.2 = ((f32[3,384,384]{2,0,1:T(4,128)}), f32[3,384,384]{2,0,1:T(4,128)}, u32[]{:S(2)}, u32[]{:S(2)}) async-start(f32[3,384,384]{2,0,1:T(4,128)} %copy.96), calls=%async_computation.2 | async-start | bytes 4718592 | tf_op jit(solution)/shard_map/all_to_all | solution.py:218
  124.8 37.2 %all-to-all-start.3 = ((f32[3,384,384]{2,0,1:T(4,128)}), f32[3,384,384]{2,0,1:T(4,128)S(1)}, u32[]{:S(2)}, u32[]{:S(2)}) async-start(f32[3,384,384]{2,0,1:T(4,128)} %copy.102), calls=%async_computation.3 | async-start | bytes 4718592 | tf_op jit(solution)/shard_map/all_to_all | solution.py:219
  183.6 5.8 copy-start.6
  202.9 37.2 %all-to-all-start.5 = ((f32[384,3,384]{2,1,0:T(4,128)}), f32[384,3,384]{2,1,0:T(4,128)S(1)}, u32[]{:S(2)}, u32[]{:S(2)}) async-start(f32[384,3,384]{2,1,0:T(4,128)} %copy.116), calls=%async_computation.5 | async-start | bytes 4718592 | tf_op jit(solution)/shard_map/all_to_all | solution.py:228
  209.5 6.9 %copy-start.7 = (f32[384,3,384]{2,0,1:T(8,128)S(1)}, f32[384,3,384]{2,0,1:T(8,128)}, u32[]{:S(2)}) copy-start(f32[384,3,384]{2,0,1:T(8,128)} %copy-done.6) | copy-start | bytes 5308420
  224.6 22.5 %copy-start.19 = (s32[3,2048]{1,0:T(4,128)S(1)}, s32[3,2048]{1,0:T(4,128)}, u32[]{:S(2)}) copy-start(s32[3,2048]{1,0:T(4,128)} %param.9) | copy-start | bytes 73732
  224.6 22.9 %copy-start.2 = (s32[128]{0:T(128)S(1)}, s32[128]{0:T(128)}, u32[]{:S(2)}) copy-start(s32[128]{0:T(128)} %param.10) | copy-start | bytes 1540
  240.1 37.7 %all-to-all-start.4 = ((f32[384,3,384]{2,1,0:T(4,128)}), f32[384,3,384]{2,1,0:T(4,128)}, u32[]{:S(2)}, u32[]{:S(2)}) async-start(f32[384,3,384]{2,1,0:T(4,128)} %copy.110), calls=%async_computation.4 | async-start | bytes 4718592 | tf_op jit(solution)/shard_map/all_to_all | solution.py:227
  297.9 36.0 %all-to-all-start.7 = ((f32[3,384,384]{2,0,1:T(4,128)}), f32[3,384,384]{2,0,1:T(4,128)}, u32[]{:S(2)}, u32[]{:S(2)}) async-start(f32[3,384,384]{2,0,1:T(4,128)} %copy.124), calls=%async_computation.7 | async-start | bytes 4718592 | tf_op jit(solution)/shard_map/all_to_all | solution.py:233
  305.7 35.9 %copy-start.11 = (f32[34,10]{0,1:T(8,128)}, f32[34,10]{0,1:T(8,128)S(1)}, u32[]{:S(2)}) copy-start(f32[34,10]{0,1:T(8,128)S(1)} %select_add_fusion) | copy-start | bytes 4084
  306.5 36.0 %copy-start.22 = (f32[10]{0:T(128)}, f32[10]{0:T(128)S(1)}, u32[]{:S(2)}) copy-start(f32[10]{0:T(128)S(1)} %get-tuple-element.4) | copy-start | bytes 124
  322.7 19.5 %copy-start.28 = (s32[16]{0:T(128)S(1)}, s32[16]{0:T(128)}, u32[]{:S(2)}) copy-start(s32[16]{0:T(128)} %get-tuple-element.5) | copy-start | bytes 196
  322.7 19.6 %copy-start.27 = (s32[16]{0:T(128)S(1)}, s32[16]{0:T(128)}, u32[]{:S(2)}) copy-start(s32[16]{0:T(128)} %get-tuple-element.6) | copy-start | bytes 196
  322.7 19.6 %copy-start.26 = (s32[16]{0:T(128)S(1)}, s32[16]{0:T(128)}, u32[]{:S(2)}) copy-start(s32[16]{0:T(128)} %get-tuple-element.7) | copy-start | bytes 196
  322.7 19.8 %copy-start.24 = (f32[10]{0:T(128)S(1)}, f32[10]{0:T(128)}, u32[]{:S(2)}) copy-start(f32[10]{0:T(128)} %get-tuple-element.3) | copy-start | bytes 124
  333.9 35.2 %all-to-all-start.6 = ((f32[3,384,384]{2,0,1:T(4,128)}), f32[3,384,384]{2,0,1:T(4,128)S(1)}, u32[]{:S(2)}, u32[]{:S(2)}) async-start(f32[3,384,384]{2,0,1:T(4,128)} %copy.120), calls=%async_computation.6 | async-start | bytes 4718592 | tf_op jit(solution)/shard_map/all_to_all | solution.py:232
  369.2 5.8 copy-start.9
  381.3 16.0 %copy-start.4 = (f32[48,24,384]{2,1,0:T(8,128)}, f32[48,24,384]{2,1,0:T(8,128)S(1)}, u32[]{:S(2)}) copy-start(f32[48,24,384]{2,1,0:T(8,128)S(1)} %subtract_multiply_fusion) | copy-start | bytes 5308420
  381.3 11.4 %collective-permute-start = (f32[1,24,384]{2,1,0:T(8,128)S(1)}, f32[1,24,384]{2,1,0:T(8,128)S(1)}, u32[]{:S(2)}, u32[]{:S(2)}) collective-permute-start(f32[1,24,384]{2,1,0:T(8,128)S(1)} %get-tuple-element.56), channel_id=1, source_target_pairs={{0,16},{16,32},{32,48},{48,64},{64,80},{80,96},{96,112},{112,0},{1... | collective-permute-start | bytes 110600 | tf_op jit(solution)/shard_map/ppermute | solution.py:27
  381.4 11.4 %collective-permute-start.1 = (f32[1,24,384]{2,1,0:T(8,128)S(1)}, f32[1,24,384]{2,1,0:T(8,128)S(1)}, u32[]{:S(2)}, u32[]{:S(2)}) collective-permute-start(f32[1,24,384]{2,1,0:T(8,128)S(1)} %get-tuple-element.57), channel_id=1, source_target_pairs={{16,0},{32,16},{48,32},{64,48},{80,64},{96,80},{112,96},{0,112},{1... | collective-permute-start | bytes 110600 | tf_op jit(solution)/shard_map/ppermute | solution.py:30
  392.9 4.5 collective-permute-start.2
  393.8 6.5 collective-permute-start.3
  402.1 151.7 %copy-start.29 = (pred[16]{0:T(512)(128)(4,1)S(1)}, pred[16]{0:T(512)(128)(4,1)}, u32[]{:S(2)}) copy-start(pred[16]{0:T(512)(128)(4,1)} %fusion.206) | copy-start | bytes 52
  402.2 168.5 %copy-start.10 = (f32[1024,100,1]{0,1,2:T(8,128)S(1)}, f32[1024,100,1]{0,1,2:T(8,128)}, u32[]{:S(2)}) copy-start(f32[1024,100,1]{0,1,2:T(8,128)} %reshape.606) | copy-start | bytes 1228804
  553.7 17.7 %copy-start.25 = (f32[10]{0:T(128)S(1)}, f32[10]{0:T(128)}, u32[]{:S(2)}) copy-start(f32[10]{0:T(128)} %get-tuple-element.3) | copy-start | bytes 124
  553.7 19.0 %copy-start.23 = (f32[10]{0:T(128)S(1)}, f32[10]{0:T(128)}, u32[]{:S(2)}) copy-start(f32[10]{0:T(128)} %copy-done.22) | copy-start | bytes 124
  554.6 15.1 %all-to-all-start.8 = ((f32[16,1,1000]{2,1,0:T(1,128)}), f32[16,1,1000]{2,1,0:T(1,128)S(1)}, u32[]{:S(2)}, u32[]{:S(2)}) async-start(f32[16,1,1000]{2,1,0:T(1,128)} %broadcast_select_fusion.1), calls=%async_computation.8 | async-start | bytes 131072 | tf_op jit(solution)/shard_map/all_to_all | solution.py:251
  578.7 5.6 copy-start.13
  579.5 11.6 %copy-start.20 = (pred[16]{0:T(512)(128)(4,1)S(1)}, pred[16]{0:T(512)(128)(4,1)}, u32[]{:S(2)}) copy-start(pred[16]{0:T(512)(128)(4,1)} %get-tuple-element.68) | copy-start | bytes 52
  580.5 13.7 %copy-start.21 = (pred[16]{0:T(512)(128)(4,1)S(1)}, pred[16]{0:T(512)(128)(4,1)}, u32[]{:S(2)}) copy-start(pred[16]{0:T(512)(128)(4,1)} %get-tuple-element.69) | copy-start | bytes 52
  580.5 14.1 %copy-start.3 = (f32[16,32,1024]{2,1,0:T(8,128)S(1)}, f32[16,32,1024]{2,1,0:T(8,128)}, u32[]{:S(2)}) copy-start(f32[16,32,1024]{2,1,0:T(8,128)} %param.7) | copy-start | bytes 6291460
  580.5 14.1 %copy-start.17 = (pred[1024]{0:T(1024)(128)(4,1)S(1)}, pred[1024]{0:T(1024)(128)(4,1)}, u32[]{:S(2)}) copy-start(pred[1024]{0:T(1024)(128)(4,1)} %get-tuple-element.81) | copy-start | bytes 3076
  580.5 14.1 %copy-start.18 = (pred[1024]{0:T(1024)(128)(4,1)S(1)}, pred[1024]{0:T(1024)(128)(4,1)}, u32[]{:S(2)}) copy-start(pred[1024]{0:T(1024)(128)(4,1)} %get-tuple-element.82) | copy-start | bytes 3076
  580.6 14.1 %copy-start.31 = (s32[32]{0:T(128)S(1)}, s32[32]{0:T(128)}, u32[]{:S(2)}) copy-start(s32[32]{0:T(128)} %iota_multiply_fusion) | copy-start | bytes 388
  580.6 10.5 %collective-permute-start.4 = (f32[16,32,32]{2,1,0:T(8,128)S(1)}, f32[16,32,32]{2,1,0:T(8,128)S(1)}, u32[]{:S(2)}, u32[]{:S(2)}) collective-permute-start(f32[16,32,32]{2,1,0:T(8,128)S(1)} %get-tuple-element.50), channel_id=1, source_target_pairs={{1,0},{2,1},{3,2},{4,3},{5,4},{6,5},{7,6},{8,7},{9,8},{10,9},{11,1... | collective-permute-start | bytes 196616 | tf_op jit(solution)/shard_map/ppermute | solution.py:18
  584.9 9.2 %collective-permute-start.5 = (f32[16,32,32]{2,1,0:T(8,128)S(1)}, f32[16,32,32]{2,1,0:T(8,128)S(1)}, u32[]{:S(2)}, u32[]{:S(2)}) collective-permute-start(f32[16,32,32]{2,1,0:T(8,128)S(1)} %get-tuple-element.51), channel_id=1, source_target_pairs={{0,1},{1,2},{2,3},{3,4},{4,5},{5,6},{6,7},{7,8},{8,9},{9,10},{10,1... | collective-permute-start | bytes 196616 | tf_op jit(solution)/shard_map/ppermute | solution.py:18
  599.0 10.4 %collective-permute-start.7 = (f32[16,32,32]{2,1,0:T(8,128)S(1)}, f32[16,32,32]{2,1,0:T(8,128)S(1)}, u32[]{:S(2)}, u32[]{:S(2)}) collective-permute-start(f32[16,32,32]{2,1,0:T(8,128)S(1)} %get-tuple-element.40), channel_id=1, source_target_pairs={{0,1},{1,2},{2,3},{3,4},{4,5},{5,6},{6,7},{7,8},{8,9},{9,10},{10,1... | collective-permute-start | bytes 196616 | tf_op jit(solution)/shard_map/ppermute | solution.py:18
  606.3 10.4 %collective-permute-start.6 = (f32[16,32,32]{2,1,0:T(8,128)S(1)}, f32[16,32,32]{2,1,0:T(8,128)S(1)}, u32[]{:S(2)}, u32[]{:S(2)}) collective-permute-start(f32[16,32,32]{2,1,0:T(8,128)S(1)} %get-tuple-element.41), channel_id=1, source_target_pairs={{1,0},{2,1},{3,2},{4,3},{5,4},{6,5},{7,6},{8,7},{9,8},{10,9},{11,1... | collective-permute-start | bytes 196616 | tf_op jit(solution)/shard_map/ppermute | solution.py:18
  621.5 10.4 %collective-permute-start.8 = (f32[16,32,32]{2,1,0:T(8,128)S(1)}, f32[16,32,32]{2,1,0:T(8,128)S(1)}, u32[]{:S(2)}, u32[]{:S(2)}) collective-permute-start(f32[16,32,32]{2,1,0:T(8,128)S(1)} %get-tuple-element.34), channel_id=1, source_target_pairs={{1,0},{2,1},{3,2},{4,3},{5,4},{6,5},{7,6},{8,7},{9,8},{10,9},{11,1... | collective-permute-start | bytes 196616 | tf_op jit(solution)/shard_map/ppermute | solution.py:18
  623.9 9.9 %collective-permute-start.9 = (f32[16,32,32]{2,1,0:T(8,128)S(1)}, f32[16,32,32]{2,1,0:T(8,128)S(1)}, u32[]{:S(2)}, u32[]{:S(2)}) collective-permute-start(f32[16,32,32]{2,1,0:T(8,128)S(1)} %get-tuple-element.35), channel_id=1, source_target_pairs={{0,1},{1,2},{2,3},{3,4},{4,5},{5,6},{6,7},{7,8},{8,9},{9,10},{10,1... | collective-permute-start | bytes 196616 | tf_op jit(solution)/shard_map/ppermute | solution.py:18
  638.3 10.8 %collective-permute-start.10 = (f32[16,32,32]{2,1,0:T(8,128)S(1)}, f32[16,32,32]{2,1,0:T(8,128)S(1)}, u32[]{:S(2)}, u32[]{:S(2)}) collective-permute-start(f32[16,32,32]{2,1,0:T(8,128)S(1)} %get-tuple-element.26), channel_id=1, source_target_pairs={{1,0},{2,1},{3,2},{4,3},{5,4},{6,5},{7,6},{8,7},{9,8},{10,9},{11,1... | collective-permute-start | bytes 196616 | tf_op jit(solution)/shard_map/ppermute | solution.py:18
  641.0 10.4 %collective-permute-start.11 = (f32[16,32,32]{2,1,0:T(8,128)S(1)}, f32[16,32,32]{2,1,0:T(8,128)S(1)}, u32[]{:S(2)}, u32[]{:S(2)}) collective-permute-start(f32[16,32,32]{2,1,0:T(8,128)S(1)} %get-tuple-element.27), channel_id=1, source_target_pairs={{0,1},{1,2},{2,3},{3,4},{4,5},{5,6},{6,7},{7,8},{8,9},{9,10},{10,1... | collective-permute-start | bytes 196616 | tf_op jit(solution)/shard_map/ppermute | solution.py:18
  657.7 10.4 %collective-permute-start.13 = (f32[16,32,32]{2,1,0:T(8,128)S(1)}, f32[16,32,32]{2,1,0:T(8,128)S(1)}, u32[]{:S(2)}, u32[]{:S(2)}) collective-permute-start(f32[16,32,32]{2,1,0:T(8,128)S(1)} %get-tuple-element.16), channel_id=1, source_target_pairs={{0,1},{1,2},{2,3},{3,4},{4,5},{5,6},{6,7},{7,8},{8,9},{9,10},{10,1... | collective-permute-start | bytes 196616 | tf_op jit(solution)/shard_map/ppermute | solution.py:18
  664.2 10.4 %collective-permute-start.12 = (f32[16,32,32]{2,1,0:T(8,128)S(1)}, f32[16,32,32]{2,1,0:T(8,128)S(1)}, u32[]{:S(2)}, u32[]{:S(2)}) collective-permute-start(f32[16,32,32]{2,1,0:T(8,128)S(1)} %get-tuple-element.17), channel_id=1, source_target_pairs={{1,0},{2,1},{3,2},{4,3},{5,4},{6,5},{7,6},{8,7},{9,8},{10,9},{11,1... | collective-permute-start | bytes 196616 | tf_op jit(solution)/shard_map/ppermute | solution.py:18
  667.2 8.2 %slice-start = ((s8[6291456]{0:T(1024)(128)(4,1)}), s8[4194304]{0:T(1024)(128)(4,1)S(1)}, s32[]{:S(2)}) async-start(s8[6291456]{0:T(1024)(128)(4,1)} %bitcast.255), calls=%async_computation.9 | async-start | bytes 8388608
  668.2 7.2 %slice-start.1 = ((s8[6291456]{0:T(1024)(128)(4,1)}), s8[2097152]{0:T(1024)(128)(4,1)S(1)}, s32[]{:S(2)}) async-start(s8[6291456]{0:T(1024)(128)(4,1)} %bitcast.255), calls=%async_computation.10 | async-start | bytes 4194304
  (9 other events, 28.8 us)
where the time goes:
time: 686 us; the launch traced here: 679 us
  local copies, waits for them, and re-layouts  227 us (33%)
  waiting for transfers between devices  182 us (27%)
  matrix products  124 us (18%)
  starting transfers between devices  113 us (16%)
  other arithmetic  30.8 us (4%)
    gather x1, local copies, waits for them, and re-layouts, cut_patches(): padded[index_first[:, :, None, None], index_second[:, None, :, None], ind...  151 us
    dot_general x20, matrix products, transform_along(): jnp.einsum(EINSUM_FORMS[axis_number], values_in, matrix, precision=HIGHES...  112 us
    ppermute x10, starting transfers between devices, from_behind(): lax.ppermute(value, axis, [(source, source + steps) for source in range(i...  41.7 us
    ppermute x10, waiting for transfers between devices, from_behind(): lax.ppermute(value, axis, [(source, source + steps) for source in range(i...  25.6 us
    all_to_all x1, waiting for transfers between devices, local(): lax.all_to_all(spectrum[1], ('px', 'py'), split_axis=1, concat_axis=0, ti...  23.2 us
    all_to_all x1, waiting for transfers between devices, local(): lax.all_to_all(spectrum[0], ('px', 'py'), split_axis=0, concat_axis=1, ti...  22.1 us
    all_to_all x1, waiting for transfers between devices, local(): lax.all_to_all(real_part, 'py', split_axis=0, concat_axis=1, tiled=True)  21.4 us
    all_to_all x1, waiting for transfers between devices, local(): lax.all_to_all(spectrum[0], 'py', split_axis=1, concat_axis=0, tiled=True)  20.7 us
  transfers between devices with their start and end apart: 23, of which 21 were waited for; matrix products, arithmetic and copies ran while one was open for 13% of the time, Pallas kernels for 0%

commit v1 on v0

--- a/solution.py
+++ b/solution.py
@@ -10,6 +10,17 @@
 HIGHEST_PRECISION = lax.Precision.HIGHEST
 RELAXATION = 6.0 / 7.0
 EINSUM_FORMS = ("abc,ad->dbc", "abc,bd->adc", "abc,cd->abd")
+
+
+def cut_along(x, dim, length):
+    before, after = (x.shape[:dim], x.shape[dim + 1 :])
+    return jnp.moveaxis(x.reshape(*before, length, -1, *after), dim, 0)
+
+
+def joined_along(blocks, dim):
+    dims = list(blocks.shape[1:])
+    dims[dim] *= blocks.shape[0]
+    return jnp.moveaxis(blocks, 0, dim).reshape(dims)
 
 
 def from_behind(value, axis, steps):
@@ -248,7 +259,14 @@
     sending_live = wanted_slot < slot_count[owner_devices]
     sending = cut_patches(padded, slot_anchor[:, global_slot], corner_first, corner_second)
     sending = jnp.where(sending_live[:, None], sending, 0.0)
-    arrived = lax.all_to_all(sending, "py", split_axis=0, concat_axis=0, tiled=True)
+    size, place = (lax.axis_size("py"), lax.axis_index("py"))
+    blocks = cut_along(sending, 0, size)
+    done = [blocks[place]]
+    for turn in range(1, size):
+        sent = blocks[place ^ turn]
+        done.append(lax.ppermute(sent, "py", [(i_2, i_2 ^ turn) for i_2 in range(size)]))
+    blocks = jnp.stack(done)[place ^ jnp.arange(size)]
+    arrived = joined_along(blocks, 0)
     patch = arrived[(place_second + positions) % size_second]
     patch_flat = patch.reshape(per_device, REG + 2, (REG + 2) * (REG + 2))
     interior, first_low, first_high, second_low, second_high, third_low, third_high = coarse_parts(

time: 686 us -> 699 us (1.019)
  starting transfers between devices: 113 us -> 135 us
    ppermute x0 -> x15, starting transfers between devices: none -> 31.4 us  [local(): lax.ppermute(sent, 'py', [(i_2, i_2 ^ turn) for i_2 in range(size)])]
    all_to_all x1 -> x0, starting transfers between devices: 9.28 us -> none  [local(): lax.all_to_all(sending, 'py', split_axis=0, concat_axis=0, tiled=True)]
  transfers between devices with their start and end apart: 23 -> 37, of which waited for: 21 -> 20; matrix products, arithmetic and copies ran while one was open for 13% -> 12% of each run, Pallas kernels for 0% -> 0%
where the time goes in v1:
time: 699 us; the launch traced here: 693 us
  local copies, waits for them, and re-layouts  224 us (32%)
  waiting for transfers between devices  178 us (25%)
  starting transfers between devices  135 us (19%)
  matrix products  124 us (18%)
  other arithmetic  29.5 us (4%)
    gather x1, local copies, waits for them, and re-layouts, cut_patches(): padded[index_first[:, :, None, None], index_second[:, None, :, None], ind...  151 us
    dot_general x20, matrix products, transform_along(): jnp.einsum(EINSUM_FORMS[axis_number], values_in, matrix, precision=HIGHES...  112 us
    ppermute x10, starting transfers between devices, from_behind(): lax.ppermute(value, axis, [(source, source + steps) for source in range(i...  41.7 us
    ppermute x15, starting transfers between devices, local(): lax.ppermute(sent, 'py', [(i_2, i_2 ^ turn) for i_2 in range(size)])  31.4 us
    ppermute x10, waiting for transfers between devices, from_behind(): lax.ppermute(value, axis, [(source, source + steps) for source in range(i...  25.6 us
    all_to_all x1, waiting for transfers between devices, local(): lax.all_to_all(spectrum[1], ('px', 'py'), split_axis=1, concat_axis=0, ti...  23.2 us
    all_to_all x1, waiting for transfers between devices, local(): lax.all_to_all(spectrum[0], ('px', 'py'), split_axis=0, concat_axis=1, ti...  22.7 us
    all_to_all x1, waiting for transfers between devices, local(): lax.all_to_all(real_part, 'py', split_axis=0, concat_axis=1, tiled=True)  21.4 us
  transfers between devices with their start and end apart: 37, of which 20 were waited for; matrix products, arithmetic and copies ran while one was open for 12% of the time, Pallas kernels for 0%

profile of v1, /device:TPU:96, one launch (start us, length us, event | category | flops | bytes accessed | tf_op | source)
XLA Modules:
  0.0 692.8 jit_solution(12589754202647125346)
XLA Ops:
  2.1 5.8 negate_bitcast_fusion
  9.6 7.8 %all-to-all-start.1 = ((f32[48,24,384]{2,1,0:T(8,128)}), f32[48,24,384]{2,1,0:T(8,128)S(1)}, u32[]{:S(2)}, u32[]{:S(2)}) async-start(f32[48,24,384]{2,1,0:T(8,128)} %copy.93), calls=%async_computation.1 | async-start | bytes 3538944 | tf_op jit(solution)/shard_map/all_to_all | solution.py:225
  17.4 5.8 fusion.38
  24.9 15.3 %all-to-all-done.1 = f32[48,24,384]{2,1,0:T(8,128)S(1)} async-done(((f32[48,24,384]{2,1,0:T(8,128)}), f32[48,24,384]{2,1,0:T(8,128)S(1)}, u32[]{:S(2)}, u32[]{:S(2)}) %all-to-all-start.1) | async-done | bytes 1769504 | tf_op jit(solution)/shard_map/all_to_all | solution.py:225
  40.2 7.7 %all-to-all-start = ((f32[48,24,384]{2,1,0:T(8,128)}), f32[48,24,384]{2,1,0:T(8,128)}, u32[]{:S(2)}, u32[]{:S(2)}) async-start(f32[48,24,384]{2,1,0:T(8,128)} %copy.89), calls=%async_computation | async-start | bytes 3538944 | tf_op jit(solution)/shard_map/all_to_all | solution.py:224
  48.1 21.4 %all-to-all-done = f32[48,24,384]{2,1,0:T(8,128)} async-done(((f32[48,24,384]{2,1,0:T(8,128)}), f32[48,24,384]{2,1,0:T(8,128)}, u32[]{:S(2)}, u32[]{:S(2)}) %all-to-all-start) | async-done | bytes 1769504 | tf_op jit(solution)/shard_map/all_to_all | solution.py:224
  71.0 5.3 fusion.71
  76.3 5.4 add_bitcast_fusion
  84.7 9.3 %all-to-all-start.2 = ((f32[3,384,384]{2,0,1:T(4,128)}), f32[3,384,384]{2,0,1:T(4,128)}, u32[]{:S(2)}, u32[]{:S(2)}) async-start(f32[3,384,384]{2,0,1:T(4,128)} %copy.96), calls=%async_computation.2 | async-start | bytes 4718592 | tf_op jit(solution)/shard_map/all_to_all | solution.py:229
  94.1 5.3 fusion.66
  99.4 5.4 subtract_bitcast_fusion
  107.5 17.3 %all-to-all-done.2 = f32[3,384,384]{2,0,1:T(4,128)} async-done(((f32[3,384,384]{2,0,1:T(4,128)}), f32[3,384,384]{2,0,1:T(4,128)}, u32[]{:S(2)}, u32[]{:S(2)}) %all-to-all-start.2) | async-done | bytes 1769504 | tf_op jit(solution)/shard_map/all_to_all | solution.py:229
  124.8 6.2 all-to-all-start.3
  134.7 4.1 all_to_all.115
  138.8 23.2 %all-to-all-done.3 = f32[3,384,384]{2,0,1:T(4,128)S(1)} async-done(((f32[3,384,384]{2,0,1:T(4,128)}), f32[3,384,384]{2,0,1:T(4,128)S(1)}, u32[]{:S(2)}, u32[]{:S(2)}) %all-to-all-start.3) | async-done | bytes 1769504 | tf_op jit(solution)/shard_map/all_to_all | solution.py:230
  166.7 5.3 fusion.64
  172.1 5.3 fusion.73
  177.4 6.2 subtract_multiply_fusion.2
  183.6 5.8 add_multiply_fusion.1
  189.4 5.5 fusion.62
  194.9 5.4 add_multiply_fusion
  202.9 6.6 all-to-all-start.5
  209.5 6.9 fusion.75
  216.4 5.4 subtract_multiply_fusion.1
  224.6 15.5 %all-to-all-done.5 = f32[384,3,384]{2,1,0:T(4,128)S(1)} async-done(((f32[384,3,384]{2,1,0:T(4,128)}), f32[384,3,384]{2,1,0:T(4,128)S(1)}, u32[]{:S(2)}, u32[]{:S(2)}) %all-to-all-start.5) | async-done | bytes 1769504 | tf_op jit(solution)/shard_map/all_to_all | solution.py:239
  240.1 7.0 %all-to-all-start.4 = ((f32[384,3,384]{2,1,0:T(4,128)}), f32[384,3,384]{2,1,0:T(4,128)}, u32[]{:S(2)}, u32[]{:S(2)}) async-start(f32[384,3,384]{2,1,0:T(4,128)} %copy.110), calls=%async_computation.4 | async-start | bytes 4718592 | tf_op jit(solution)/shard_map/all_to_all | solution.py:238
  255.1 22.7 %all-to-all-done.4 = f32[384,3,384]{2,1,0:T(4,128)} async-done(((f32[384,3,384]{2,1,0:T(4,128)}), f32[384,3,384]{2,1,0:T(4,128)}, u32[]{:S(2)}, u32[]{:S(2)}) %all-to-all-start.4) | async-done | bytes 1769504 | tf_op jit(solution)/shard_map/all_to_all | solution.py:238
  284.2 5.3 fusion.60
  289.5 5.4 multiply_bitcast_fusion.1
  297.9 5.9 all-to-all-start.7
  309.0 5.3 fusion.77
  314.3 5.4 multiply_bitcast_fusion.2
  322.5 11.4 %all-to-all-done.7 = f32[3,384,384]{2,0,1:T(4,128)} async-done(((f32[3,384,384]{2,0,1:T(4,128)}), f32[3,384,384]{2,0,1:T(4,128)}, u32[]{:S(2)}, u32[]{:S(2)}) %all-to-all-start.7) | async-done | bytes 1769504 | tf_op jit(solution)/shard_map/all_to_all | solution.py:244
  333.9 6.9 all-to-all-start.6
  348.3 20.7 %all-to-all-done.6 = f32[3,384,384]{2,0,1:T(4,128)S(1)} async-done(((f32[3,384,384]{2,0,1:T(4,128)}), f32[3,384,384]{2,0,1:T(4,128)S(1)}, u32[]{:S(2)}, u32[]{:S(2)}) %all-to-all-start.6) | async-done | bytes 1769504 | tf_op jit(solution)/shard_map/all_to_all | solution.py:243
  369.1 5.8 fusion.68
  375.0 5.9 subtract_multiply_fusion
  395.9 151.5 %gather_fusion.2 = f32[16000]{0:T(1024)S(1)} fusion(f32[50,26,384]{2,1,0:T(8,128)S(1)} %pad_maximum_fusion.8, s32[16000]{0:T(1024)S(1)} %reshape.595), kind=kCustom, calls=%fused_computation.2 | custom fusion | bytes 320000 | tf_op jit(solution)/shard_map/gather | solution.py:197
  550.9 7.7 %collective-permute-start.16 = (f32[1,1000]{1,0:T(1,128)S(1)}, f32[1,1000]{1,0:T(1,128)S(1)}, u32[]{:S(2)}, u32[]{:S(2)}) collective-permute-start(f32[1,1000]{1,0:T(1,128)S(1)} %get-tuple-element.64), channel_id=1, source_target_pairs={{0,13},{1,12},{2,15},{3,14},{4,9},{5,8},{6,11},{7,10},{8,5},{9,4},... | collective-permute-start | bytes 12008 | tf_op jit(solution)/shard_map/ppermute | solution.py:267
  558.7 5.0 collective-permute-start.13
  563.7 4.4 collective-permute-start.11
  598.4 5.7 collective-permute-start.20
  612.6 6.5 collective-permute-start.22
  623.1 7.3 %collective-permute-done.21 = f32[16,32,32]{2,1,0:T(8,128)S(1)} collective-permute-done((f32[16,32,32]{2,1,0:T(8,128)S(1)}, f32[16,32,32]{2,1,0:T(8,128)S(1)}, u32[]{:S(2)}, u32[]{:S(2)}) %collective-permute-start.21) | collective-permute-done | bytes 65568 | tf_op jit(solution)/shard_map/ppermute | solution.py:29
  637.5 6.0 collective-permute-start.24
  654.6 6.7 collective-permute-start.26
  671.3 6.5 collective-permute-start.28
  681.8 6.4 collective-permute-done.27
  (243 shorter events, 156.2 us)
Async XLA Ops:
  9.6 30.6 %all-to-all-start.1 = ((f32[48,24,384]{2,1,0:T(8,128)}), f32[48,24,384]{2,1,0:T(8,128)S(1)}, u32[]{:S(2)}, u32[]{:S(2)}) async-start(f32[48,24,384]{2,1,0:T(8,128)} %copy.93), calls=%async_computation.1 | async-start | bytes 3538944 | tf_op jit(solution)/shard_map/all_to_all | solution.py:225
  40.2 29.3 %all-to-all-start = ((f32[48,24,384]{2,1,0:T(8,128)}), f32[48,24,384]{2,1,0:T(8,128)}, u32[]{:S(2)}, u32[]{:S(2)}) async-start(f32[48,24,384]{2,1,0:T(8,128)} %copy.89), calls=%async_computation | async-start | bytes 3538944 | tf_op jit(solution)/shard_map/all_to_all | solution.py:224
  84.7 40.1 %all-to-all-start.2 = ((f32[3,384,384]{2,0,1:T(4,128)}), f32[3,384,384]{2,0,1:T(4,128)}, u32[]{:S(2)}, u32[]{:S(2)}) async-start(f32[3,384,384]{2,0,1:T(4,128)} %copy.96), calls=%async_computation.2 | async-start | bytes 4718592 | tf_op jit(solution)/shard_map/all_to_all | solution.py:229
  124.8 37.2 %all-to-all-start.3 = ((f32[3,384,384]{2,0,1:T(4,128)}), f32[3,384,384]{2,0,1:T(4,128)S(1)}, u32[]{:S(2)}, u32[]{:S(2)}) async-start(f32[3,384,384]{2,0,1:T(4,128)} %copy.102), calls=%async_computation.3 | async-start | bytes 4718592 | tf_op jit(solution)/shard_map/all_to_all | solution.py:230
  202.9 37.2 %all-to-all-start.5 = ((f32[384,3,384]{2,1,0:T(4,128)}), f32[384,3,384]{2,1,0:T(4,128)S(1)}, u32[]{:S(2)}, u32[]{:S(2)}) async-start(f32[384,3,384]{2,1,0:T(4,128)} %copy.116), calls=%async_computation.5 | async-start | bytes 4718592 | tf_op jit(solution)/shard_map/all_to_all | solution.py:239
  224.6 22.5 %copy-start.19 = (s32[3,2048]{1,0:T(4,128)S(1)}, s32[3,2048]{1,0:T(4,128)}, u32[]{:S(2)}) copy-start(s32[3,2048]{1,0:T(4,128)} %param.9) | copy-start | bytes 73732
  224.6 22.9 %copy-start.2 = (s32[128]{0:T(128)S(1)}, s32[128]{0:T(128)}, u32[]{:S(2)}) copy-start(s32[128]{0:T(128)} %param.10) | copy-start | bytes 1540
  240.1 37.7 %all-to-all-start.4 = ((f32[384,3,384]{2,1,0:T(4,128)}), f32[384,3,384]{2,1,0:T(4,128)}, u32[]{:S(2)}, u32[]{:S(2)}) async-start(f32[384,3,384]{2,1,0:T(4,128)} %copy.110), calls=%async_computation.4 | async-start | bytes 4718592 | tf_op jit(solution)/shard_map/all_to_all | solution.py:238
  297.9 36.0 %all-to-all-start.7 = ((f32[3,384,384]{2,0,1:T(4,128)}), f32[3,384,384]{2,0,1:T(4,128)}, u32[]{:S(2)}, u32[]{:S(2)}) async-start(f32[3,384,384]{2,0,1:T(4,128)} %copy.124), calls=%async_computation.7 | async-start | bytes 4718592 | tf_op jit(solution)/shard_map/all_to_all | solution.py:244
  306.4 34.4 %copy-start.11 = (f32[34,10]{0,1:T(8,128)}, f32[34,10]{0,1:T(8,128)S(1)}, u32[]{:S(2)}) copy-start(f32[34,10]{0,1:T(8,128)S(1)} %select_add_fusion) | copy-start | bytes 4084
  322.5 19.2 %copy-start.22 = (f32[10]{0:T(128)S(1)}, f32[10]{0:T(128)}, u32[]{:S(2)}) copy-start(f32[10]{0:T(128)} %get-tuple-element.4) | copy-start | bytes 124
  322.5 19.2 %copy-start.24 = (f32[10]{0:T(128)S(1)}, f32[10]{0:T(128)}, u32[]{:S(2)}) copy-start(f32[10]{0:T(128)} %get-tuple-element.3) | copy-start | bytes 124
  333.9 35.2 %all-to-all-start.6 = ((f32[3,384,384]{2,0,1:T(4,128)}), f32[3,384,384]{2,0,1:T(4,128)S(1)}, u32[]{:S(2)}, u32[]{:S(2)}) async-start(f32[3,384,384]{2,0,1:T(4,128)} %copy.120), calls=%async_computation.6 | async-start | bytes 4718592 | tf_op jit(solution)/shard_map/all_to_all | solution.py:243
  380.9 5.4 collective-permute-start
  381.0 5.4 collective-permute-start.1
  386.5 4.5 collective-permute-start.2
  387.5 6.5 collective-permute-start.3
  395.8 151.7 %copy-start.30 = (pred[16]{0:T(512)(128)(4,1)S(1)}, pred[16]{0:T(512)(128)(4,1)}, u32[]{:S(2)}) copy-start(pred[16]{0:T(512)(128)(4,1)} %fusion.227) | copy-start | bytes 52
  395.8 175.8 %copy-start.3 = (s32[128]{0:T(128)S(1)}, s32[128]{0:T(128)}, u32[]{:S(2)}) copy-start(s32[128]{0:T(128)} %param.10) | copy-start | bytes 1540
  395.8 184.5 %copy-start.16 = (f32[32,10,10]{0,1,2:T(8,128)S(1)}, f32[32,10,10]{0,1,2:T(8,128)}, u32[]{:S(2)}) copy-start(f32[32,10,10]{0,1,2:T(8,128)} %get-tuple-element.78) | copy-start | bytes 38404
  395.8 184.5 %copy-start.15 = (f32[32,10,10]{0,2,1:T(8,128)S(1)}, f32[32,10,10]{0,2,1:T(8,128)}, u32[]{:S(2)}) copy-start(f32[32,10,10]{0,2,1:T(8,128)} %get-tuple-element.79) | copy-start | bytes 38404
  395.8 184.5 %copy-start.14 = (f32[32,10,10]{0,2,1:T(8,128)S(1)}, f32[32,10,10]{0,2,1:T(8,128)}, u32[]{:S(2)}) copy-start(f32[32,10,10]{0,2,1:T(8,128)} %get-tuple-element.82) | copy-start | bytes 38404
  395.9 184.5 %copy-start.13 = (f32[32,10,10]{0,1,2:T(8,128)S(1)}, f32[32,10,10]{0,1,2:T(8,128)}, u32[]{:S(2)}) copy-start(f32[32,10,10]{0,1,2:T(8,128)} %get-tuple-element.83) | copy-start | bytes 38404
  547.6 11.0 %collective-permute-start.18 = (f32[1,1000]{1,0:T(1,128)S(1)}, f32[1,1000]{1,0:T(1,128)S(1)}, u32[]{:S(2)}, u32[]{:S(2)}) collective-permute-start(f32[1,1000]{1,0:T(1,128)S(1)} %get-tuple-element.62), channel_id=1, source_target_pairs={{0,15},{1,14},{2,13},{3,12},{4,11},{5,10},{6,9},{7,8},{8,7},{9,6},... | collective-permute-start | bytes 12008 | tf_op jit(solution)/shard_map/ppermute | solution.py:267
  549.1 14.6 %collective-permute-start.17 = (f32[1,1000]{1,0:T(1,128)S(1)}, f32[1,1000]{1,0:T(1,128)S(1)}, u32[]{:S(2)}, u32[]{:S(2)}) collective-permute-start(f32[1,1000]{1,0:T(1,128)S(1)} %get-tuple-element.63), channel_id=1, source_target_pairs={{0,14},{1,15},{2,12},{3,13},{4,10},{5,11},{6,8},{7,9},{8,6},{9,7},... | collective-permute-start | bytes 12008 | tf_op jit(solution)/shard_map/ppermute | solution.py:267
  550.9 12.8 %collective-permute-start.16 = (f32[1,1000]{1,0:T(1,128)S(1)}, f32[1,1000]{1,0:T(1,128)S(1)}, u32[]{:S(2)}, u32[]{:S(2)}) collective-permute-start(f32[1,1000]{1,0:T(1,128)S(1)} %get-tuple-element.64), channel_id=1, source_target_pairs={{0,13},{1,12},{2,15},{3,14},{4,9},{5,8},{6,11},{7,10},{8,5},{9,4},... | collective-permute-start | bytes 12008 | tf_op jit(solution)/shard_map/ppermute | solution.py:267
  558.6 9.5 %collective-permute-start.15 = (f32[1,1000]{1,0:T(1,128)S(1)}, f32[1,1000]{1,0:T(1,128)S(1)}, u32[]{:S(2)}, u32[]{:S(2)}) collective-permute-start(f32[1,1000]{1,0:T(1,128)S(1)} %get-tuple-element.65), channel_id=1, source_target_pairs={{0,12},{1,13},{2,14},{3,15},{4,8},{5,9},{6,10},{7,11},{8,4},{9,5},... | collective-permute-start | bytes 12008 | tf_op jit(solution)/shard_map/ppermute | solution.py:267
  558.6 10.1 %collective-permute-start.14 = (f32[1,1000]{1,0:T(1,128)S(1)}, f32[1,1000]{1,0:T(1,128)S(1)}, u32[]{:S(2)}, u32[]{:S(2)}) collective-permute-start(f32[1,1000]{1,0:T(1,128)S(1)} %get-tuple-element.66), channel_id=1, source_target_pairs={{0,11},{1,10},{2,9},{3,8},{4,15},{5,14},{6,13},{7,12},{8,3},{9,2},... | collective-permute-start | bytes 12008 | tf_op jit(solution)/shard_map/ppermute | solution.py:267
  558.7 13.6 %collective-permute-start.13 = (f32[1,1000]{1,0:T(1,128)S(1)}, f32[1,1000]{1,0:T(1,128)S(1)}, u32[]{:S(2)}, u32[]{:S(2)}) collective-permute-start(f32[1,1000]{1,0:T(1,128)S(1)} %get-tuple-element.67), channel_id=1, source_target_pairs={{0,10},{1,11},{2,8},{3,9},{4,14},{5,15},{6,12},{7,13},{8,2},{9,3},... | collective-permute-start | bytes 12008 | tf_op jit(solution)/shard_map/ppermute | solution.py:267
  563.7 10.1 %collective-permute-start.12 = (f32[1,1000]{1,0:T(1,128)S(1)}, f32[1,1000]{1,0:T(1,128)S(1)}, u32[]{:S(2)}, u32[]{:S(2)}) collective-permute-start(f32[1,1000]{1,0:T(1,128)S(1)} %get-tuple-element.68), channel_id=1, source_target_pairs={{0,9},{1,8},{2,11},{3,10},{4,13},{5,12},{6,15},{7,14},{8,1},{9,0},... | collective-permute-start | bytes 12008 | tf_op jit(solution)/shard_map/ppermute | solution.py:267
  563.7 11.5 %collective-permute-start.11 = (f32[1,1000]{1,0:T(1,128)S(1)}, f32[1,1000]{1,0:T(1,128)S(1)}, u32[]{:S(2)}, u32[]{:S(2)}) collective-permute-start(f32[1,1000]{1,0:T(1,128)S(1)} %get-tuple-element.69), channel_id=1, source_target_pairs={{0,8},{1,9},{2,10},{3,11},{4,12},{5,13},{6,14},{7,15},{8,0},{9,1},... | collective-permute-start | bytes 12008 | tf_op jit(solution)/shard_map/ppermute | solution.py:267
  568.1 7.7 %collective-permute-start.10 = (f32[1,1000]{1,0:T(1,128)S(1)}, f32[1,1000]{1,0:T(1,128)S(1)}, u32[]{:S(2)}, u32[]{:S(2)}) collective-permute-start(f32[1,1000]{1,0:T(1,128)S(1)} %get-tuple-element.70), channel_id=1, source_target_pairs={{0,7},{1,6},{2,5},{3,4},{4,3},{5,2},{6,1},{7,0},{8,15},{9,14},{10,... | collective-permute-start | bytes 12008 | tf_op jit(solution)/shard_map/ppermute | solution.py:267
  568.8 9.1 %collective-permute-start.9 = (f32[1,1000]{1,0:T(1,128)S(1)}, f32[1,1000]{1,0:T(1,128)S(1)}, u32[]{:S(2)}, u32[]{:S(2)}) collective-permute-start(f32[1,1000]{1,0:T(1,128)S(1)} %get-tuple-element.71), channel_id=1, source_target_pairs={{0,6},{1,7},{2,4},{3,5},{4,2},{5,3},{6,0},{7,1},{8,14},{9,15},{10,... | collective-permute-start | bytes 12008 | tf_op jit(solution)/shard_map/ppermute | solution.py:267
  572.3 10.4 %collective-permute-start.8 = (f32[1,1000]{1,0:T(1,128)S(1)}, f32[1,1000]{1,0:T(1,128)S(1)}, u32[]{:S(2)}, u32[]{:S(2)}) collective-permute-start(f32[1,1000]{1,0:T(1,128)S(1)} %get-tuple-element.72), channel_id=1, source_target_pairs={{0,5},{1,4},{2,7},{3,6},{4,1},{5,0},{6,3},{7,2},{8,13},{9,12},{10,... | collective-permute-start | bytes 12008 | tf_op jit(solution)/shard_map/ppermute | solution.py:267
  573.8 8.9 %collective-permute-start.7 = (f32[1,1000]{1,0:T(1,128)S(1)}, f32[1,1000]{1,0:T(1,128)S(1)}, u32[]{:S(2)}, u32[]{:S(2)}) collective-permute-start(f32[1,1000]{1,0:T(1,128)S(1)} %get-tuple-element.73), channel_id=1, source_target_pairs={{0,4},{1,5},{2,6},{3,7},{4,0},{5,1},{6,2},{7,3},{8,12},{9,13},{10,... | collective-permute-start | bytes 12008 | tf_op jit(solution)/shard_map/ppermute | solution.py:267
  575.2 7.5 %collective-permute-start.6 = (f32[1,1000]{1,0:T(1,128)S(1)}, f32[1,1000]{1,0:T(1,128)S(1)}, u32[]{:S(2)}, u32[]{:S(2)}) collective-permute-start(f32[1,1000]{1,0:T(1,128)S(1)} %get-tuple-element.74), channel_id=1, source_target_pairs={{0,3},{1,2},{2,1},{3,0},{4,7},{5,6},{6,5},{7,4},{8,11},{9,10},{10,... | collective-permute-start | bytes 12008 | tf_op jit(solution)/shard_map/ppermute | solution.py:267
  575.8 6.9 collective-permute-start.5
  577.8 4.9 collective-permute-start.4
  594.2 10.5 %collective-permute-start.19 = (f32[16,32,32]{2,1,0:T(8,128)S(1)}, f32[16,32,32]{2,1,0:T(8,128)S(1)}, u32[]{:S(2)}, u32[]{:S(2)}) collective-permute-start(f32[16,32,32]{2,1,0:T(8,128)S(1)} %get-tuple-element.50), channel_id=1, source_target_pairs={{1,0},{2,1},{3,2},{4,3},{5,4},{6,5},{7,6},{8,7},{9,8},{10,9},{11,1... | collective-permute-start | bytes 196616 | tf_op jit(solution)/shard_map/ppermute | solution.py:29
  598.4 9.4 %collective-permute-start.20 = (f32[16,32,32]{2,1,0:T(8,128)S(1)}, f32[16,32,32]{2,1,0:T(8,128)S(1)}, u32[]{:S(2)}, u32[]{:S(2)}) collective-permute-start(f32[16,32,32]{2,1,0:T(8,128)S(1)} %get-tuple-element.51), channel_id=1, source_target_pairs={{0,1},{1,2},{2,3},{3,4},{4,5},{5,6},{6,7},{7,8},{8,9},{9,10},{10,1... | collective-permute-start | bytes 196616 | tf_op jit(solution)/shard_map/ppermute | solution.py:29
  612.6 10.4 %collective-permute-start.22 = (f32[16,32,32]{2,1,0:T(8,128)S(1)}, f32[16,32,32]{2,1,0:T(8,128)S(1)}, u32[]{:S(2)}, u32[]{:S(2)}) collective-permute-start(f32[16,32,32]{2,1,0:T(8,128)S(1)} %get-tuple-element.40), channel_id=1, source_target_pairs={{0,1},{1,2},{2,3},{3,4},{4,5},{5,6},{6,7},{7,8},{8,9},{9,10},{10,1... | collective-permute-start | bytes 196616 | tf_op jit(solution)/shard_map/ppermute | solution.py:29
  619.9 10.4 %collective-permute-start.21 = (f32[16,32,32]{2,1,0:T(8,128)S(1)}, f32[16,32,32]{2,1,0:T(8,128)S(1)}, u32[]{:S(2)}, u32[]{:S(2)}) collective-permute-start(f32[16,32,32]{2,1,0:T(8,128)S(1)} %get-tuple-element.41), channel_id=1, source_target_pairs={{1,0},{2,1},{3,2},{4,3},{5,4},{6,5},{7,6},{8,7},{9,8},{10,9},{11,1... | collective-permute-start | bytes 196616 | tf_op jit(solution)/shard_map/ppermute | solution.py:29
  635.1 10.4 %collective-permute-start.23 = (f32[16,32,32]{2,1,0:T(8,128)S(1)}, f32[16,32,32]{2,1,0:T(8,128)S(1)}, u32[]{:S(2)}, u32[]{:S(2)}) collective-permute-start(f32[16,32,32]{2,1,0:T(8,128)S(1)} %get-tuple-element.34), channel_id=1, source_target_pairs={{1,0},{2,1},{3,2},{4,3},{5,4},{6,5},{7,6},{8,7},{9,8},{10,9},{11,1... | collective-permute-start | bytes 196616 | tf_op jit(solution)/shard_map/ppermute | solution.py:29
  637.5 9.9 %collective-permute-start.24 = (f32[16,32,32]{2,1,0:T(8,128)S(1)}, f32[16,32,32]{2,1,0:T(8,128)S(1)}, u32[]{:S(2)}, u32[]{:S(2)}) collective-permute-start(f32[16,32,32]{2,1,0:T(8,128)S(1)} %get-tuple-element.35), channel_id=1, source_target_pairs={{0,1},{1,2},{2,3},{3,4},{4,5},{5,6},{6,7},{7,8},{8,9},{9,10},{10,1... | collective-permute-start | bytes 196616 | tf_op jit(solution)/shard_map/ppermute | solution.py:29
  651.9 10.8 %collective-permute-start.25 = (f32[16,32,32]{2,1,0:T(8,128)S(1)}, f32[16,32,32]{2,1,0:T(8,128)S(1)}, u32[]{:S(2)}, u32[]{:S(2)}) collective-permute-start(f32[16,32,32]{2,1,0:T(8,128)S(1)} %get-tuple-element.26), channel_id=1, source_target_pairs={{1,0},{2,1},{3,2},{4,3},{5,4},{6,5},{7,6},{8,7},{9,8},{10,9},{11,1... | collective-permute-start | bytes 196616 | tf_op jit(solution)/shard_map/ppermute | solution.py:29
  654.6 10.4 %collective-permute-start.26 = (f32[16,32,32]{2,1,0:T(8,128)S(1)}, f32[16,32,32]{2,1,0:T(8,128)S(1)}, u32[]{:S(2)}, u32[]{:S(2)}) collective-permute-start(f32[16,32,32]{2,1,0:T(8,128)S(1)} %get-tuple-element.27), channel_id=1, source_target_pairs={{0,1},{1,2},{2,3},{3,4},{4,5},{5,6},{6,7},{7,8},{8,9},{9,10},{10,1... | collective-permute-start | bytes 196616 | tf_op jit(solution)/shard_map/ppermute | solution.py:29
  671.3 10.4 %collective-permute-start.28 = (f32[16,32,32]{2,1,0:T(8,128)S(1)}, f32[16,32,32]{2,1,0:T(8,128)S(1)}, u32[]{:S(2)}, u32[]{:S(2)}) collective-permute-start(f32[16,32,32]{2,1,0:T(8,128)S(1)} %get-tuple-element.16), channel_id=1, source_target_pairs={{0,1},{1,2},{2,3},{3,4},{4,5},{5,6},{6,7},{7,8},{8,9},{9,10},{10,1... | collective-permute-start | bytes 196616 | tf_op jit(solution)/shard_map/ppermute | solution.py:29
  677.9 10.4 %collective-permute-start.27 = (f32[16,32,32]{2,1,0:T(8,128)S(1)}, f32[16,32,32]{2,1,0:T(8,128)S(1)}, u32[]{:S(2)}, u32[]{:S(2)}) collective-permute-start(f32[16,32,32]{2,1,0:T(8,128)S(1)} %get-tuple-element.17), channel_id=1, source_target_pairs={{1,0},{2,1},{3,2},{4,3},{5,4},{6,5},{7,6},{8,7},{9,8},{10,9},{11,1... | collective-permute-start | bytes 196616 | tf_op jit(solution)/shard_map/ppermute | solution.py:29
  (22 other events, 215.8 us)
